TPU v7x, 256 devices: a whole 4x4x8 slice. The times are simulated.
256 devices in a mesh: expert: 32 (over z, y), etp: 8 (over x, core).
Axes of the slice: x: 4, y: 4, z: 8, core: 2. Of those that a mesh axis runs over, the one named last changes fastest.
Arguments:
- tokens: bfloat16 [32768, 2560], P(('expert', 'etp')), may hold values from -6 to 6
- grad_out: bfloat16 [32768, 2560], P(('expert', 'etp')), may hold values from -6 to 6
- router_weight: bfloat16 [2560, 32], replicated, may hold values from -0.125 to 0.125
- expert_choice: int32 [32768, 1], P(('expert', 'etp')), may hold values from 0 to 31; in each aligned block of 128 rows (0 to 127, 128 to 255, ...) at most 6 rows name the same one
- gate_pre: bfloat16 [32, 1536, 4096], P('expert', None, 'etp'), may hold values from -6 to 6
- up_pre: bfloat16 [32, 1536, 4096], P('expert', None, 'etp'), may hold values from -6 to 6
- w_gate: bfloat16 [32, 2560, 4096], P('expert', None, 'etp'), may hold values from -0.125 to 0.125
- w_up: bfloat16 [32, 2560, 4096], P('expert', None, 'etp'), may hold values from -0.125 to 0.125
- w_down: bfloat16 [32, 4096, 2560], P('expert', 'etp'), may hold values from -0.09375 to 0.09375
Outputs:
- token_grad: bfloat16 [32768, 2560], P(('expert', 'etp'))
- router_grad: float32 [2560, 32], replicated
Inputs may be any that keep to these rules, and one draw needn't show every extreme that they name: `expert_choice`: within the 128 tokens of one device no expert is chosen more than 6 times, and in every draw some expert is chosen exactly 6 times by the tokens of some device.
All inputs are finite; a program needn't handle non-finite values.
Results may differ from a plain program's by a relative error of at most 0.015.
Values may be sent and summed in bfloat16 or wider, within the bound.
No kernel may reach another device: no remote copies, remote signals or barrier semaphores. Data moves between devices by JAX's collectives and lax.ppermute only.
A program may use at most 128 MiB of HBM per device.

v0:
```python
import jax
import jax.numpy as jnp
from jax import lax
from jax.sharding import PartitionSpec as P


def local(tokens, grad_out, router_weight, expert_choice, gate_pre, up_pre, w_gate, w_up, w_down):
    width = tokens.shape[1]
    experts = router_weight.shape[1]
    n_expert = lax.axis_size("expert")
    n_etp = lax.axis_size("etp")
    capacity = gate_pre.shape[1] // (n_expert * n_etp)
    contract = (((1,), (1,)), ((), ()))
    chosen_ids = expert_choice[:, 0]
    picked = chosen_ids[:, None] == jnp.arange(experts, dtype=jnp.int32)[None, :]
    logits = jnp.dot(tokens, router_weight, preferred_element_type=jnp.float32)
    score = jax.nn.sigmoid(jnp.sum(jnp.where(picked, logits, 0.0), axis=1))
    counts = picked.astype(jnp.int32)
    earlier = jnp.cumsum(counts, axis=0) - counts
    position = jnp.sum(earlier * counts, axis=1)
    target = chosen_ids * capacity + position
    placed = jnp.arange(experts * capacity, dtype=jnp.int32)[:, None] == target[None, :]
    onehot = placed.astype(jnp.bfloat16)
    outgoing = jnp.dot(onehot, grad_out, preferred_element_type=jnp.float32).astype(jnp.bfloat16)
    own = lax.all_to_all(outgoing, "expert", split_axis=0, concat_axis=0, tiled=True)
    arrived = lax.all_gather(own, "etp", axis=0, tiled=True)
    d_hidden = lax.dot_general(arrived, w_down[0], contract, preferred_element_type=jnp.float32)
    gate_f = gate_pre[0].astype(jnp.float32)
    up_f = up_pre[0].astype(jnp.float32)
    sig = jax.nn.sigmoid(gate_f)
    d_gate = (d_hidden * up_f * sig * (1.0 + gate_f * (1.0 - sig))).astype(jnp.bfloat16)
    d_up = (d_hidden * gate_f * sig).astype(jnp.bfloat16)
    terms = (
        lax.dot_general(d_gate, w_gate[0], contract, preferred_element_type=jnp.float32)
        + lax.dot_general(d_up, w_up[0], contract, preferred_element_type=jnp.float32)
    ).astype(jnp.bfloat16)
    summed = lax.psum_scatter(terms, "etp", scatter_dimension=0, tiled=True)
    returned = lax.all_to_all(summed, "expert", split_axis=0, concat_axis=0, tiled=True)
    fetched = lax.dot_general(
        onehot, returned, (((0,), (0,)), ((), ())), preferred_element_type=jnp.float32
    )
    inputs = tokens.astype(jnp.float32)
    d_logit = jnp.sum(inputs * fetched, axis=1) * score * (1.0 - score)
    column = lax.dot_general(
        picked.astype(jnp.bfloat16), router_weight, contract, preferred_element_type=jnp.float32
    )
    token_grad = (score[:, None] * fetched + d_logit[:, None] * column).astype(jnp.bfloat16)
    weighted = jnp.where(picked, d_logit[:, None], 0.0)
    local_terms = lax.dot_general(
        weighted,
        inputs,
        (((0,), (0,)), ((), ())),
        precision=lax.Precision.HIGHEST,
        preferred_element_type=jnp.float32,
    )
    mine = lax.all_to_all(
        local_terms.reshape(n_etp, experts // n_etp, width),
        "etp",
        split_axis=0,
        concat_axis=0,
        tiled=True,
    )
    mine = jnp.sum(mine, axis=0)
    mine = lax.psum(mine, "expert")
    router_grad = lax.all_gather(mine, "etp", axis=0, tiled=True).T
    return (token_grad, router_grad)


def solution(mesh):
    placed = (
        P(("expert", "etp"), None),
        P(("expert", "etp"), None),
        P(),
        P(("expert", "etp"), None),
        P("expert", None, "etp"),
        P("expert", None, "etp"),
        P("expert", None, "etp"),
        P("expert", None, "etp"),
        P("expert", "etp", None),
    )
    return jax.shard_map(
        local,
        mesh=mesh,
        in_specs=placed,
        out_specs=(P(("expert", "etp"), None), P()),
        check_vma=False,
    )
```

profile of v0, /device:TPU:1, one launch (start us, length us, event | category | flops | bytes accessed | tf_op | source)
XLA Modules:
  0.0 423.1 jit_solution(13606596880845416231)
XLA Ops:
  7.2 0.0 copy-start
  7.2 0.0 all-gather.3.cloned.1.call-start
  7.2 0.8 fusion.29
  8.0 0.1 copy.15
  8.1 0.2 reduce_window_sum.11
  8.3 0.1 copy.16
  8.4 0.7 select_reduce_fusion
  9.1 0.7 multiply_add_fusion
  9.7 2.5 convolution_convert_fusion
  12.2 2.3 all_to_all.19
  14.4 46.0 %all_to_all.29 = bf16[32,6,2560]{2,1,0:T(8,128)(2,1)} all-to-all(bf16[32,6,2560]{2,1,0:T(8,128)(2,1)} %all_to_all.19), channel_id=1, replica_groups=mesh['expert'=32,'etp'=8] {'expert'}, dimensions={0} | all-to-all | bytes 1966080 | tf_op jit(solution)/shard_map/all_to_all | solution.py:25
  60.4 2.3 all_to_all.21
  62.7 0.0 all-gather.3.cloned.1.call-update
  62.7 0.0 reduce-scatter.2.cloned.1.call-start
  62.8 47.8 %all-gather.3.cloned.1.call-done = bf16[1536,2560]{1,0:T(8,128)(2,1)} async-done(((bf16[192,2560]{1,0:T(8,128)(2,1)}), bf16[1536,2560]{1,0:T(8,128)(2,1)}) %all-gather.3.cloned.1.call-update) | async-done | bytes 7864336 | tf_op jit(solution)/shard_map/all_gather | solution.py:26
  110.6 0.0 copy-start.4
  110.6 0.0 copy-start.5
  110.6 7.5 %fusion.14 = f32[1536,512]{1,0:T(8,128)S(1)} fusion(bf16[1536,2560]{1,0:T(8,128)(2,1)} %all-gather.3.cloned.1.call-done, bf16[1,512,2560]{2,1,0:T(8,128)(2,1)} %param.17), kind=kOutput, calls=%fused_computation.21 | convolution fusion | flops 4026531840 | bytes 13631488 | tf_op jit(solution)/shard_map/dot_general | solution.py:27
  118.1 0.0 copy-start.6
  118.1 1.7 copy-done.6
  119.8 0.0 copy-done
  119.8 0.0 copy-done.4
  119.8 0.0 copy-done.5
  119.8 9.8 %fusion.12 = f32[1536,2560]{1,0:T(8,128)} fusion(bf16[1,2560,512]{2,1,0:T(8,128)(2,1)S(1)} %copy-done, f32[1536,512]{1,0:T(8,128)S(1)} %fusion.14, bf16[1,1536,512]{2,1,0:T(8,128)(2,1)S(1)} %copy-done.4, bf16[1,1536,512]{2,1,0:T(8,128)(2,1)S(1)} %copy-done.5), kind=kOutput, calls=%fused_computation.19 | convolution fusion | flops 4035969024 | bytes 24641536 | tf_op jit(solution)/shard_map/dot_general | solution.py:34
  129.6 15.2 %add_convert_fusion = bf16[1536,2560]{1,0:T(8,128)(2,1)} fusion(f32[1536,2560]{1,0:T(8,128)} %fusion.12, bf16[1,2560,512]{2,1,0:T(8,128)(2,1)} %param.16, f32[1536,512]{1,0:T(8,128)} %copy-done.6, bf16[1,1536,512]{2,1,0:T(8,128)(2,1)} %param.13), kind=kOutput, calls=%fused_computation | convolution fusion | flops 4039901184 | bytes 30932992 | tf_op jit(solution)/shard_map/dot_general | solution.py:35
  144.9 0.0 reduce-scatter.2.cloned.1.call-update
  144.9 0.0 copy-start.1
  144.9 0.0 copy-start.2
  144.9 0.0 copy-start.3
  144.9 51.8 %reduce-scatter.2.cloned.1.call-done = bf16[192,2560]{1,0:T(8,128)(2,1)} async-done(((bf16[1536,2560]{1,0:T(8,128)(2,1)}), bf16[192,2560]{1,0:T(8,128)(2,1)}) %reduce-scatter.2.cloned.1.call-update) | async-done | bytes 983056 | tf_op jit(solution)/shard_map/reduce_scatter | solution.py:37
  196.8 2.3 all_to_all.22
  199.0 9.7 %all-to-all-start.1 = ((bf16[32,6,2560]{2,1,0:T(8,128)(2,1)}), bf16[32,6,2560]{2,1,0:T(8,128)(2,1)}, u32[]{:S(2)}, u32[]{:S(2)}) async-start(bf16[32,6,2560]{2,1,0:T(8,128)(2,1)} %all_to_all.22), calls=%async_computation.2 | async-start | bytes 2621440 | tf_op jit(solution)/shard_map/all_to_all | solution.py:38
  208.7 0.0 copy-done.1
  208.7 0.0 copy-done.2
  208.8 0.0 copy-done.3
  208.8 0.3 fusion.23
  209.1 30.4 %all-to-all-done.1 = bf16[32,6,2560]{2,1,0:T(8,128)(2,1)} async-done(((bf16[32,6,2560]{2,1,0:T(8,128)(2,1)}), bf16[32,6,2560]{2,1,0:T(8,128)(2,1)}, u32[]{:S(2)}, u32[]{:S(2)}) %all-to-all-start.1) | async-done | bytes 983072 | tf_op jit(solution)/shard_map/all_to_all | solution.py:38
  239.5 2.2 all_to_all.24
  241.7 2.7 multiply_reduce_fusion
  244.4 1.1 fusion.27
  245.5 1.8 reshape.36
  247.3 7.3 %all-to-all-start.2 = ((f32[8,4,2560]{2,1,0:T(4,128)}), f32[8,4,2560]{2,1,0:T(4,128)S(1)}, u32[]{:S(2)}, u32[]{:S(2)}) async-start(f32[8,4,2560]{2,1,0:T(4,128)} %reshape.36), calls=%async_computation.3 | async-start | bytes 655360 | tf_op jit(solution)/shard_map/all_to_all | solution.py:56
  254.6 2.5 fusion.1
  257.1 4.6 %all-to-all-done.2 = f32[8,4,2560]{2,1,0:T(4,128)S(1)} async-done(((f32[8,4,2560]{2,1,0:T(4,128)}), f32[8,4,2560]{2,1,0:T(4,128)S(1)}, u32[]{:S(2)}, u32[]{:S(2)}) %all-to-all-start.2) | async-done | bytes 327712 | tf_op jit(solution)/shard_map/all_to_all | solution.py:56
  261.7 0.1 reduce_sum.39
  261.8 112.4 %psum.7 = f32[4,2560]{1,0:T(4,128)S(1)} all-reduce(f32[4,2560]{1,0:T(4,128)S(1)} %reduce_sum.39), channel_id=1, replica_groups=mesh['expert'=32,'etp'=8] {'expert'}, use_global_device_ids=true, to_apply=%region_6.7 | all-reduce | flops 10240 | bytes 81920 | tf_op jit(solution)/shard_map/psum | solution.py:64
  374.2 41.3 %all-gather = f32[8,4,2560]{2,1,0:T(4,128)S(1)} all-gather(f32[1,4,2560]{2,1,0:T(4,128)S(1)} %bitcast.37), channel_id=1, replica_groups=mesh['expert'=32,'etp'=8] {'etp'}, dimensions={0}, use_global_device_ids=true | all-gather | bytes 368640 | tf_op jit(solution)/shard_map/all_gather | solution.py:65
  415.5 0.8 reshape.40
  (1 shorter events, 0.0 us)
Async XLA Ops:
  7.2 112.6 %copy-start = (bf16[1,2560,512]{2,1,0:T(8,128)(2,1)S(1)}, bf16[1,2560,512]{2,1,0:T(8,128)(2,1)}, u32[]{:S(2)}) copy-start(bf16[1,2560,512]{2,1,0:T(8,128)(2,1)} %param.15) | copy-start | bytes 7864324
  7.2 103.4 %all-gather.3.cloned.1.call-start = ((), (), s32[]{:S(2)}) async-start(), calls=%async_computation.4 | async-start | bytes 8847360 | tf_op jit(solution)/shard_map/all_gather | solution.py:26
  62.7 134.0 %reduce-scatter.2.cloned.1.call-start = ((), (), s32[]{:S(2)}) async-start(), calls=%async_computation.5 | async-start | bytes 8847360 | tf_op jit(solution)/shard_map/reduce_scatter | solution.py:37
  110.6 9.3 %copy-start.4 = (bf16[1,1536,512]{2,1,0:T(8,128)(2,1)S(1)}, bf16[1,1536,512]{2,1,0:T(8,128)(2,1)}, u32[]{:S(2)}) copy-start(bf16[1,1536,512]{2,1,0:T(8,128)(2,1)} %param.14) | copy-start | bytes 4718596
  110.6 9.3 %copy-start.5 = (bf16[1,1536,512]{2,1,0:T(8,128)(2,1)S(1)}, bf16[1,1536,512]{2,1,0:T(8,128)(2,1)}, u32[]{:S(2)}) copy-start(bf16[1,1536,512]{2,1,0:T(8,128)(2,1)} %param.13) | copy-start | bytes 4718596
  118.1 1.7 copy-start.6
  144.9 63.8 %copy-start.1 = (bf16[128,2560]{1,0:T(8,128)(2,1)S(1)}, bf16[128,2560]{1,0:T(8,128)(2,1)}, u32[]{:S(2)}) copy-start(bf16[128,2560]{1,0:T(8,128)(2,1)} %param.9) | copy-start | bytes 1966084
  144.9 63.8 %copy-start.2 = (bf16[2560,32]{0,1:T(8,128)(2,1)S(1)}, bf16[2560,32]{0,1:T(8,128)(2,1)}, u32[]{:S(2)}) copy-start(bf16[2560,32]{0,1:T(8,128)(2,1)} %param.11) | copy-start | bytes 491524
  144.9 63.8 %copy-start.3 = (s32[128,1]{0,1:T(1,128)S(1)}, s32[128,1]{0,1:T(1,128)}, u32[]{:S(2)}) copy-start(s32[128,1]{0,1:T(1,128)} %param.12) | copy-start | bytes 1540
  199.0 40.4 %all-to-all-start.1 = ((bf16[32,6,2560]{2,1,0:T(8,128)(2,1)}), bf16[32,6,2560]{2,1,0:T(8,128)(2,1)}, u32[]{:S(2)}, u32[]{:S(2)}) async-start(bf16[32,6,2560]{2,1,0:T(8,128)(2,1)} %all_to_all.22), calls=%async_computation.2 | async-start | bytes 2621440 | tf_op jit(solution)/shard_map/all_to_all | solution.py:38
  247.3 14.4 %all-to-all-start.2 = ((f32[8,4,2560]{2,1,0:T(4,128)}), f32[8,4,2560]{2,1,0:T(4,128)S(1)}, u32[]{:S(2)}, u32[]{:S(2)}) async-start(f32[8,4,2560]{2,1,0:T(4,128)} %reshape.36), calls=%async_computation.3 | async-start | bytes 655360 | tf_op jit(solution)/shard_map/all_to_all | solution.py:56
Sparse Core Ops, SparseCore 0:
  62.9 47.6 all-gather.2
  145.0 51.6 reduce-scatter.1
where the time goes:
time: 424 us; the launch traced here: 423 us
  blocking collectives  200 us (47%)
  waiting for transfers between devices  135 us (32%)
  matrix products  41.7 us (10%)
  starting transfers between devices  17.1 us (4%)
  between operations  14.1 us (3%)
  local copies, waits for them, and re-layouts  13.6 us (3%)
    psum x1, blocking collectives, local(): mine = lax.psum(mine, 'expert')  112 us
    reduce_scatter x1, waiting for transfers between devices, local(): summed = lax.psum_scatter(terms, 'etp', scatter_dimension=0, tiled=True)  51.8 us
    all_gather x1, waiting for transfers between devices, local(): arrived = lax.all_gather(own, 'etp', axis=0, tiled=True)  47.8 us
    all_to_all x1, blocking collectives, local(): lax.all_to_all(outgoing, 'expert', split_axis=0, concat_axis=0, tiled=True)  46 us
    all_gather x1, blocking collectives, local(): router_grad = lax.all_gather(mine, 'etp', axis=0, tiled=True).T  41.3 us
    all_to_all x1, waiting for transfers between devices, local(): lax.all_to_all(summed, 'expert', split_axis=0, concat_axis=0, tiled=True)  30.4 us
    dot_general x1, matrix products, local(): lax.dot_general(d_up, w_up[0], contract, preferred_element_type=jnp.float32)  15.2 us
    dot_general x1, matrix products, local(): lax.dot_general(d_gate, w_gate[0], contract, preferred_element_type=jnp.f...  9.81 us
  transfers between devices with their start and end apart: 4, of which 4 were waited for; matrix products, arithmetic and copies ran while one was open for 1% of the time, Pallas kernels for 0%

commit v1 on v0

--- a/solution.py
+++ b/solution.py
@@ -23,7 +23,9 @@
     onehot = placed.astype(jnp.bfloat16)
     outgoing = jnp.dot(onehot, grad_out, preferred_element_type=jnp.float32).astype(jnp.bfloat16)
     own = lax.all_to_all(outgoing, "expert", split_axis=0, concat_axis=0, tiled=True)
-    arrived = lax.all_gather(own, "etp", axis=0, tiled=True)
+    arrived = jnp.concatenate(
+        lax.all_to_all(jnp.stack([own] * lax.axis_size("etp")), "etp", 0, 0), axis=0
+    )
     d_hidden = lax.dot_general(arrived, w_down[0], contract, preferred_element_type=jnp.float32)
     gate_f = gate_pre[0].astype(jnp.float32)
     up_f = up_pre[0].astype(jnp.float32)

time: 424 us -> 461 us (1.087)
  blocking collectives: 200 us -> 295 us
  waiting for transfers between devices: 135 us -> 81 us
    all_to_all x0 -> x1, blocking collectives: none -> 95.9 us  [local(): lax.all_to_all(jnp.stack([own] * lax.axis_size('etp')), 'etp', 0, 0)]
    all_gather x1 -> x0, waiting for transfers between devices: 47.8 us -> none  [local(): arrived = lax.all_gather(own, 'etp', axis=0, tiled=True)]
    reduce_scatter x1, waiting for transfers between devices: 51.8 us -> 46.1 us  [local(): summed = lax.psum_scatter(terms, 'etp', scatter_dimension=0, tiled=True)]
  transfers between devices with their start and end apart: 4 -> 3, of which waited for: 4 -> 3; matrix products, arithmetic and copies ran while one was open for 1% -> 1% of each run, Pallas kernels for 0% -> 0%
where the time goes in v1:
time: 461 us; the launch traced here: 460 us
  blocking collectives  295 us (64%)
  waiting for transfers between devices  81 us (18%)
  matrix products  37.3 us (8%)
  starting transfers between devices  16.9 us (4%)
  between operations  14.2 us (3%)
  local copies, waits for them, and re-layouts  13.5 us (3%)
    psum x1, blocking collectives, local(): mine = lax.psum(mine, 'expert')  112 us
    all_to_all x1, blocking collectives, local(): lax.all_to_all(jnp.stack([own] * lax.axis_size('etp')), 'etp', 0, 0)  95.9 us
    reduce_scatter x1, waiting for transfers between devices, local(): summed = lax.psum_scatter(terms, 'etp', scatter_dimension=0, tiled=True)  46.1 us
    all_to_all x1, blocking collectives, local(): lax.all_to_all(outgoing, 'expert', split_axis=0, concat_axis=0, tiled=True)  45.9 us
    all_gather x1, blocking collectives, local(): router_grad = lax.all_gather(mine, 'etp', axis=0, tiled=True).T  41.3 us
    all_to_all x1, waiting for transfers between devices, local(): lax.all_to_all(summed, 'expert', split_axis=0, concat_axis=0, tiled=True)  30.4 us
    dot_general x1, matrix products, local(): lax.dot_general(d_up, w_up[0], contract, preferred_element_type=jnp.float32)  15.2 us
    dot_general x1, matrix products, local(): lax.dot_general(d_gate, w_gate[0], contract, preferred_element_type=jnp.f...  9.88 us
  transfers between devices with their start and end apart: 3, of which 3 were waited for; matrix products, arithmetic and copies ran while one was open for 1% of the time, Pallas kernels for 0%

profile of v1, /device:TPU:1, one launch (start us, length us, event | category | flops | bytes accessed | tf_op | source)
XLA Modules:
  0.0 460.5 jit_solution(9700229709786381388)
XLA Ops:
  7.2 0.0 copy-start
  7.2 0.0 reduce-scatter.2.cloned.1.call-start
  7.2 0.8 fusion.29
  8.0 0.1 copy.15
  8.1 0.2 reduce_window_sum.11
  8.3 0.1 copy.16
  8.4 0.7 select_reduce_fusion
  9.1 0.7 multiply_add_fusion
  9.7 2.5 convolution_convert_fusion
  12.2 2.3 all_to_all.20
  14.5 45.9 %all_to_all.31 = bf16[32,6,2560]{2,1,0:T(8,128)(2,1)} all-to-all(bf16[32,6,2560]{2,1,0:T(8,128)(2,1)} %all_to_all.20), channel_id=1, replica_groups=mesh['expert'=32,'etp'=8] {'expert'}, dimensions={0} | all-to-all | bytes 1966080 | tf_op jit(solution)/shard_map/all_to_all | solution.py:25
  60.4 2.2 stack.4
  62.6 1.9 stack.5
  64.5 0.0 copy-start.5
  64.5 95.9 %all_to_all.32 = bf16[8,192,2560]{2,1,0:T(8,128)(2,1)S(1)} all-to-all(bf16[8,192,2560]{2,1,0:T(8,128)(2,1)S(1)} %stack.5), channel_id=1, replica_groups=mesh['expert'=32,'etp'=8] {'etp'}, dimensions={0} | all-to-all | bytes 15728640 | tf_op jit(solution)/shard_map/all_to_all | solution.py:27
  160.5 0.0 copy-done.5
  160.5 0.0 copy-start.6
  160.5 0.0 copy-start.7
  160.5 4.3 fusion.14
  164.8 0.0 copy-start.8
  164.8 1.7 copy-done.8
  166.5 0.0 copy-done
  166.5 0.0 copy-done.6
  166.5 0.0 copy-done.7
  166.5 9.9 %fusion.12 = f32[1536,2560]{1,0:T(8,128)} fusion(bf16[1,2560,512]{2,1,0:T(8,128)(2,1)S(1)} %copy-done, f32[1536,512]{1,0:T(8,128)S(1)} %fusion.14, bf16[1,1536,512]{2,1,0:T(8,128)(2,1)S(1)} %copy-done.6, bf16[1,1536,512]{2,1,0:T(8,128)(2,1)S(1)} %copy-done.7), kind=kOutput, calls=%fused_computation.19 | convolution fusion | flops 4035969024 | bytes 24641536 | tf_op jit(solution)/shard_map/dot_general | solution.py:36
  176.3 15.2 %add_convert_fusion = bf16[1536,2560]{1,0:T(8,128)(2,1)} fusion(f32[1536,2560]{1,0:T(8,128)} %fusion.12, bf16[1,2560,512]{2,1,0:T(8,128)(2,1)} %param.16, f32[1536,512]{1,0:T(8,128)} %copy-done.8, bf16[1,1536,512]{2,1,0:T(8,128)(2,1)} %param.13), kind=kOutput, calls=%fused_computation | convolution fusion | flops 4039901184 | bytes 30932992 | tf_op jit(solution)/shard_map/dot_general | solution.py:37
  191.6 0.0 reduce-scatter.2.cloned.1.call-update
  191.6 0.0 copy-start.2
  191.6 0.0 copy-start.3
  191.6 0.0 copy-start.4
  191.7 46.1 %reduce-scatter.2.cloned.1.call-done = bf16[192,2560]{1,0:T(8,128)(2,1)} async-done(((bf16[1536,2560]{1,0:T(8,128)(2,1)}), bf16[192,2560]{1,0:T(8,128)(2,1)}) %reduce-scatter.2.cloned.1.call-update) | async-done | bytes 983056 | tf_op jit(solution)/shard_map/reduce_scatter | solution.py:39
  237.7 2.3 all_to_all.23
  240.0 9.6 %all-to-all-start.2 = ((bf16[32,6,2560]{2,1,0:T(8,128)(2,1)}), bf16[32,6,2560]{2,1,0:T(8,128)(2,1)S(1)}, u32[]{:S(2)}, u32[]{:S(2)}) async-start(bf16[32,6,2560]{2,1,0:T(8,128)(2,1)} %all_to_all.23), calls=%async_computation.3 | async-start | bytes 2621440 | tf_op jit(solution)/shard_map/all_to_all | solution.py:40
  249.5 0.0 copy-done.2
  249.5 0.0 copy-done.3
  249.6 0.0 copy-done.4
  249.6 0.3 fusion.23
  249.9 30.4 %all-to-all-done.2 = bf16[32,6,2560]{2,1,0:T(8,128)(2,1)S(1)} async-done(((bf16[32,6,2560]{2,1,0:T(8,128)(2,1)}), bf16[32,6,2560]{2,1,0:T(8,128)(2,1)S(1)}, u32[]{:S(2)}, u32[]{:S(2)}) %all-to-all-start.2) | async-done | bytes 983072 | tf_op jit(solution)/shard_map/all_to_all | solution.py:40
  280.3 0.4 all_to_all.25
  280.6 1.5 multiply_reduce_fusion
  282.1 0.0 copy-start.1
  282.1 1.1 fusion.27
  283.2 1.8 reshape.43
  285.0 7.3 %all-to-all-start.3 = ((f32[8,4,2560]{2,1,0:T(4,128)}), f32[8,4,2560]{2,1,0:T(4,128)S(1)}, u32[]{:S(2)}, u32[]{:S(2)}) async-start(f32[8,4,2560]{2,1,0:T(4,128)} %reshape.43), calls=%async_computation.4 | async-start | bytes 655360 | tf_op jit(solution)/shard_map/all_to_all | solution.py:58
  292.3 2.5 fusion.1
  294.9 4.6 all-to-all-done.3
  299.4 0.1 reduce_sum.39
  299.5 112.0 %psum.7 = f32[4,2560]{1,0:T(4,128)S(1)} all-reduce(f32[4,2560]{1,0:T(4,128)S(1)} %reduce_sum.39), channel_id=1, replica_groups=mesh['expert'=32,'etp'=8] {'expert'}, use_global_device_ids=true, to_apply=%region_6.7 | all-reduce | flops 10240 | bytes 81920 | tf_op jit(solution)/shard_map/psum | solution.py:66
  411.5 41.3 %all-gather = f32[8,4,2560]{2,1,0:T(4,128)S(1)} all-gather(f32[1,4,2560]{2,1,0:T(4,128)S(1)} %bitcast.39), channel_id=1, replica_groups=mesh['expert'=32,'etp'=8] {'etp'}, dimensions={0}, use_global_device_ids=true | all-gather | bytes 368640 | tf_op jit(solution)/shard_map/all_gather | solution.py:67
  452.8 0.8 reshape.47
  453.6 0.0 copy-done.1
  (1 shorter events, 0.0 us)
Async XLA Ops:
  7.2 159.3 %copy-start = (bf16[1,2560,512]{2,1,0:T(8,128)(2,1)S(1)}, bf16[1,2560,512]{2,1,0:T(8,128)(2,1)}, u32[]{:S(2)}) copy-start(bf16[1,2560,512]{2,1,0:T(8,128)(2,1)} %param.15) | copy-start | bytes 7864324
  7.2 230.5 %reduce-scatter.2.cloned.1.call-start = ((), (), s32[]{:S(2)}) async-start(), calls=%async_computation.5 | async-start | bytes 8847360 | tf_op jit(solution)/shard_map/reduce_scatter | solution.py:39
  64.5 95.9 %copy-start.5 = (bf16[1,512,2560]{2,1,0:T(8,128)(2,1)S(1)}, bf16[1,512,2560]{2,1,0:T(8,128)(2,1)}, u32[]{:S(2)}) copy-start(bf16[1,512,2560]{2,1,0:T(8,128)(2,1)} %param.17) | copy-start | bytes 7864324
  160.5 6.0 %copy-start.6 = (bf16[1,1536,512]{2,1,0:T(8,128)(2,1)S(1)}, bf16[1,1536,512]{2,1,0:T(8,128)(2,1)}, u32[]{:S(2)}) copy-start(bf16[1,1536,512]{2,1,0:T(8,128)(2,1)} %param.14) | copy-start | bytes 4718596
  160.5 6.0 %copy-start.7 = (bf16[1,1536,512]{2,1,0:T(8,128)(2,1)S(1)}, bf16[1,1536,512]{2,1,0:T(8,128)(2,1)}, u32[]{:S(2)}) copy-start(bf16[1,1536,512]{2,1,0:T(8,128)(2,1)} %param.13) | copy-start | bytes 4718596
  164.8 1.7 copy-start.8
  191.6 57.9 %copy-start.2 = (bf16[128,2560]{1,0:T(8,128)(2,1)S(1)}, bf16[128,2560]{1,0:T(8,128)(2,1)}, u32[]{:S(2)}) copy-start(bf16[128,2560]{1,0:T(8,128)(2,1)} %param.9) | copy-start | bytes 1966084
  191.6 57.9 %copy-start.3 = (bf16[2560,32]{0,1:T(8,128)(2,1)S(1)}, bf16[2560,32]{0,1:T(8,128)(2,1)}, u32[]{:S(2)}) copy-start(bf16[2560,32]{0,1:T(8,128)(2,1)} %param.11) | copy-start | bytes 491524
  191.6 57.9 %copy-start.4 = (s32[128,1]{0,1:T(1,128)S(1)}, s32[128,1]{0,1:T(1,128)}, u32[]{:S(2)}) copy-start(s32[128,1]{0,1:T(1,128)} %param.12) | copy-start | bytes 1540
  240.0 40.3 %all-to-all-start.2 = ((bf16[32,6,2560]{2,1,0:T(8,128)(2,1)}), bf16[32,6,2560]{2,1,0:T(8,128)(2,1)S(1)}, u32[]{:S(2)}, u32[]{:S(2)}) async-start(bf16[32,6,2560]{2,1,0:T(8,128)(2,1)} %all_to_all.23), calls=%async_computation.3 | async-start | bytes 2621440 | tf_op jit(solution)/shard_map/all_to_all | solution.py:40
  282.1 171.5 %copy-start.1 = (bf16[1,2560,512]{2,1,0:T(8,128)(2,1)S(1)}, bf16[1,2560,512]{2,1,0:T(8,128)(2,1)}, u32[]{:S(2)}) copy-start(bf16[1,2560,512]{2,1,0:T(8,128)(2,1)} %param.15) | copy-start | bytes 7864324
  285.0 14.4 %all-to-all-start.3 = ((f32[8,4,2560]{2,1,0:T(4,128)}), f32[8,4,2560]{2,1,0:T(4,128)S(1)}, u32[]{:S(2)}, u32[]{:S(2)}) async-start(f32[8,4,2560]{2,1,0:T(4,128)} %reshape.43), calls=%async_computation.4 | async-start | bytes 655360 | tf_op jit(solution)/shard_map/all_to_all | solution.py:58
Sparse Core Ops, SparseCore 0:
  191.7 45.9 reduce-scatter.1
